TPU v7x, 32 devices: a whole 2x2x4 slice. The times are simulated.
32 devices in a mesh: grp: 4 (over y, x), blk: 8 (over z, core).
Axes of the slice: x: 2, y: 2, z: 4, core: 2. Of those that a mesh axis runs over, the one named last changes fastest.
Arguments:
- estimate: float32 [32, 256, 256], P('blk'), may hold values from 0.25 to 4
- measured: bfloat16 [6, 256, 32, 256], P(None, 'blk'), may hold values from 0.25 to 4
- tile_plane: int32 [6, 256], P(None, 'blk'), may hold values from 0 to 31, as said below
- tile_strip: int32 [6, 256], P(None, 'blk'), may hold values from 0 to 7, as said below
- view_group: int32 [6], replicated, may hold values from 0 to 3, as said below
- kernel_cols: float32 [6, 3, 31], replicated, may hold values from 0.002 to 0.1
- kernel_rows: float32 [6, 3, 31], replicated, may hold values from 0.002 to 0.1
- kernel_planes: float32 [6, 3, 31], replicated, may hold values from 0.002 to 0.1
Outputs:
- updated: float32 [32, 256, 256], P('blk')
Inputs may be any that keep to these rules, and one draw needn't show every extreme that they name: For each view the pairs (tile_plane, tile_strip) name every plane and strip exactly once; the 32 tiles of one view on one device of blk hold exactly 4 tiles of every block of 4 consecutive planes and exactly 4 tiles of every strip. `tile_strip`: see tile_plane. `view_group`: every group has at least one view and at most 2; some group has exactly 2.
All inputs are finite; a program needn't handle non-finite values.
Results may differ from a plain program's by a relative error of at most 0.0003.
Values may be sent and summed in bfloat16 or wider, within the bound.
A program may use at most 128 MiB of HBM per device.

v0:
```python
import jax
import jax.numpy as jnp
from jax import lax
from jax.sharding import PartitionSpec as P

VSLOT = 2
HIGH = lax.Precision.HIGH


def band(taps, rows, cols, lead):
    width = taps.shape[-1]
    shift = lax.broadcasted_iota(jnp.int32, (rows, cols), 1) - lax.broadcasted_iota(
        jnp.int32, (rows, cols), 0
    )
    shift = shift - lead + width // 2
    out = jnp.zeros(taps.shape[:-1] + (rows, cols), jnp.float32)
    for t in range(width):
        out = jnp.where(shift == t, taps[..., t, None, None], out)
    return out


def shards(
    estimate, measured, tile_plane, tile_strip, view_group, kernel_cols, kernel_rows, kernel_planes
):
    cz, ny, nx = estimate.shape
    blocks = lax.axis_size("blk")
    groups = lax.axis_size("grp")
    nz = cz * blocks
    py = ny // blocks
    half = kernel_rows.shape[-1] // 2
    lead = -(-half // 8) * 8
    ext = py + 2 * lead
    tiles = measured.shape[1]
    per = tiles // blocks
    matches = (view_group == lax.axis_index("grp")).astype(jnp.int32)
    ranking = jnp.cumsum(matches) - matches
    members = jnp.sum(matches).astype(jnp.float32)
    ids = jnp.arange(view_group.shape[0], dtype=jnp.int32)
    picked = [matches * (ranking == s).astype(jnp.int32) for s in range(VSLOT)]
    chosen = [jnp.sum(p * ids) for p in picked]
    weights = jnp.stack([jnp.sum(p).astype(jnp.float32) / members for p in picked])
    padded = jnp.pad(estimate, ((0, 0), (lead, lead), (0, 0)))
    windows = jnp.stack([padded[:, j * py : j * py + ext] for j in range(blocks)])
    pencil = lax.all_to_all(windows, "blk", 0, 0, tiled=True).reshape(nz, ext, nx)
    pick = lambda a: jnp.stack([lax.dynamic_index_in_dim(a, c, 0, keepdims=False) for c in chosen])
    pieces, planes, strips = (pick(measured), pick(tile_plane), pick(tile_strip))
    hits = (strips[:, :, None] == jnp.arange(blocks, dtype=jnp.int32)).astype(jnp.int32)
    before = jnp.cumsum(hits, axis=1) - hits
    positions = strips * per + jnp.sum(before * hits, axis=2)
    order = positions[:, None, :] == jnp.arange(tiles, dtype=jnp.int32)[None, :, None]
    send_planes = jnp.sum(jnp.where(order, planes[:, None, :], 0), axis=2)
    send = jnp.einsum("vpi,viyx->pvyx", order.astype(jnp.bfloat16), pieces)
    got = lax.all_to_all(send, "blk", 0, 0, tiled=True)
    got_planes = lax.all_to_all(send_planes.T, "blk", 0, 0, tiled=True)
    place = (got_planes[None] == jnp.arange(nz, dtype=jnp.int32)[:, None, None]).astype(
        jnp.bfloat16
    )
    observed = jnp.einsum("ptv,tvyx->vpyx", place, got).astype(jnp.float32)
    kc, kr, kp = (pick(kernel_cols), pick(kernel_rows), pick(kernel_planes))
    bx = band(kc, nx, nx, 0)
    by = band(kr, py, ext, lead)
    bz = band(kp, nz, nz, 0)
    byw = by * weights[:, None, None, None]
    t = jnp.einsum("zmx,vrim->vrzix", pencil, by, precision=HIGH)
    t = jnp.einsum("vrzix,vrnx->vrzin", t, bx, precision=HIGH)
    blurred = jnp.einsum("vrzin,vrpz->vpin", t, bz, precision=HIGH)
    ratios = observed / blurred
    a = jnp.einsum("vpin,vrpz->vrzin", ratios, bz, precision=HIGH)
    a = jnp.einsum("vrzin,vrnx->vrzix", a, bx, precision=HIGH)
    wide = jnp.einsum("vrzix,vrim->zmx", a, byw, precision=HIGH)
    chunk = min(py, lead)
    average = wide[:, lead : lead + py]
    for d in range(1, lead // chunk + 1):
        up = wide[:, lead + py + (d - 1) * chunk : lead + py + d * chunk]
        down = wide[:, lead - d * chunk : lead - (d - 1) * chunk]
        up = lax.ppermute(up, "blk", [(i, i + d) for i in range(blocks - d)])
        down = lax.ppermute(down, "blk", [(i, i - d) for i in range(d, blocks)])
        rest = py - chunk
        average = (
            average
            + jnp.pad(up, ((0, 0), (0, rest), (0, 0)))
            + jnp.pad(down, ((0, 0), (rest, 0), (0, 0)))
        )
    logs = jnp.log(average)
    logs = lax.all_to_all(logs.reshape(blocks, cz, py, nx), "blk", 0, 0, tiled=True)
    summed = lax.psum(logs, "grp")
    summed = jnp.transpose(summed, (1, 0, 2, 3)).reshape(cz, ny, nx)
    return estimate * jnp.exp(summed / groups)


def solution(mesh):
    in_specs = (
        P("blk", None, None),
        P(None, "blk", None, None),
        P(None, "blk"),
        P(None, "blk"),
        P(),
        P(),
        P(),
        P(),
    )
    return jax.shard_map(
        shards, mesh=mesh, in_specs=in_specs, out_specs=P("blk", None, None), check_vma=False
    )
```

profile of v0, /device:TPU:0, one launch (start us, length us, event | category | flops | bytes accessed | tf_op | source)
XLA Modules:
  0.0 310.7 jit_solution(15629209679689618100)
XLA Ops:
  7.4 1.4 fusion.249
  15.5 6.4 %all-to-all-start = ((s32[8,4,2]{1,2,0:T(2,128)}), s32[8,4,2]{1,2,0:T(2,128)S(1)}, u32[]{:S(2)}, u32[]{:S(2)}) async-start(s32[8,4,2]{1,2,0:T(2,128)} %copy.106), calls=%async_computation | async-start | bytes 16384 | tf_op jit(solution)/shard_map/all_to_all | solution.py:54
  77.9 1.3 constant_dynamic-slice_fusion.3
  80.2 1.6 copy.110
  84.4 5.1 %all-to-all-start.1 = ((bf16[32,2,32,256]{3,2,1,0:T(8,128)(2,1)}), bf16[32,2,32,256]{3,2,1,0:T(8,128)(2,1)S(1)}, u32[]{:S(2)}, u32[]{:S(2)}) async-start(bf16[32,2,32,256]{3,2,1,0:T(8,128)(2,1)} %copy.110), calls=%async_computation.1 | async-start | bytes 2097152 | tf_op jit(solution)/shard_map/all_to_all | solution.py:53
  95.4 20.7 %all-to-all-done.1 = bf16[32,2,32,256]{3,2,1,0:T(8,128)(2,1)S(1)} async-done(((bf16[32,2,32,256]{3,2,1,0:T(8,128)(2,1)}), bf16[32,2,32,256]{3,2,1,0:T(8,128)(2,1)S(1)}, u32[]{:S(2)}, u32[]{:S(2)}) %all-to-all-start.1) | async-done | bytes 1048608 | tf_op jit(solution)/shard_map/all_to_all | solution.py:53
  116.1 1.0 copy-done.2
  117.1 3.6 %all-to-all-start.2 = ((f32[8,4,64,256]{3,2,1,0:T(8,128)}), f32[8,4,64,256]{3,2,1,0:T(8,128)S(1)}, u32[]{:S(2)}, u32[]{:S(2)}) async-start(f32[8,4,64,256]{3,2,1,0:T(8,128)} %fusion.19), calls=%async_computation.2 | async-start | bytes 4194304 | tf_op jit(solution)/shard_map/all_to_all | solution.py:44
  132.7 1.4 eq.730
  134.0 2.9 fusion.14
  137.0 32.7 %all-to-all-done.2 = f32[8,4,64,256]{3,2,1,0:T(8,128)S(1)} async-done(((f32[8,4,64,256]{3,2,1,0:T(8,128)}), f32[8,4,64,256]{3,2,1,0:T(8,128)S(1)}, u32[]{:S(2)}, u32[]{:S(2)}) %all-to-all-start.2) | async-done | bytes 2097184 | tf_op jit(solution)/shard_map/all_to_all | solution.py:44
  169.9 4.2 %convolution_bitcast_fusion = f32[2,3,32,32,256]{4,3,2,1,0:T(8,128)S(1)} fusion(f32[32,64,256,1,1]{2,1,0,4,3:T(8,128)S(1)} %bitcast.177, f32[2,3]{0,1:T(4,128)} %bitcast.239, pred[32,64]{1,0:T(8,128)(4,1)S(1)} %get-tuple-element.121, f32[2,3]{0,1:T(4,128)} %bitcast.237, pred[32,64]{1,0:T(8,128)(4,1)S(1)} %get-tuple-element.122, f32[2,3]{0,1:T(4,128)} %bitcast.235, ...), kind=kOutput, calls=%fused_computation.4 | convolution fusion | flops 604360704 | bytes 8452840 | tf_op jit(solution)/shard_map/zmx,vrim->vrzix/dot_general | solution.py:64
  174.5 10.7 %fusion.2 = f32[2,3,32,32,256]{4,2,1,3,0:T(8,128)S(1)} fusion(f32[2,3,32,32,256]{4,3,2,1,0:T(8,128)S(1)} %convolution_bitcast_fusion, f32[2,3]{0,1:T(4,128)} %bitcast.302, pred[256,256]{1,0:T(8,128)(4,1)S(1)} %get-tuple-element.151, f32[2,3]{0,1:T(4,128)} %bitcast.300, pred[256,256]{1,0:T(8,128)(4,1)S(1)} %get-tuple-element.152, f32[2,3]{0,1:T(4,128)} %bitcast.298, ...), kind=kOutput, calls=%fused_computation.2 | convolution fusion | flops 2428108800 | bytes 14615272 | tf_op jit(solution)/shard_map/vrzix,vrnx->vrzin/dot_general | solution.py:65
  185.6 3.2 %fusion.51 = f32[2,32,32,256,1]{3,1,4,2,0:T(8,128)S(1)} fusion(f32[2,3,32,32,256]{4,2,1,3,0:T(8,128)S(1)} %fusion.2, f32[2,3]{1,0:T(2,128)} %get-tuple-element.34, f32[2,3]{1,0:T(2,128)} %get-tuple-element.35, f32[2,3]{1,0:T(2,128)} %get-tuple-element.33, f32[2,3]{1,0:T(2,128)} %get-tuple-element.32, f32[2,3]{1,0:T(2,128)} %get-tuple-element.31, ...), kind=kOutput, calls=%fused_computation.68 | convolution fusion | flops 302180352 | bytes 8421096 | tf_op jit(solution)/shard_map/vrzin,vrpz->vpin/dot_general | solution.py:66
  189.0 2.9 fusion.4
  192.4 11.0 %fusion = f32[2,3,32,32,256]{4,3,0,2,1:T(8,128)S(1)} fusion(f32[2,3,32,32,256]{4,2,3,1,0:T(8,128)S(1)} %fusion.4, f32[2,3]{0,1:T(4,128)} %bitcast.303, f32[2,3]{0,1:T(4,128)} %bitcast.301, f32[2,3]{0,1:T(4,128)} %bitcast.299, f32[2,3]{0,1:T(4,128)} %bitcast.297, f32[2,3]{0,1:T(4,128)} %bitcast.295, f32[2,3]{0,1:T(4,128)} %bitcast.293, f32[2,3]{0,1:T(4,128)} %bitcast.291, ...), kind=kOutput, calls=%fused_computation | convolution fusion | flops 2428108800 | bytes 14615272 | tf_op jit(solution)/shard_map/vrzin,vrnx->vrzix/dot_general | solution.py:69
  203.7 3.6 %convolution_bitcast_fusion.1 = f32[32,64,256]{2,1,0:T(8,128)S(1)} fusion(f32[2,3,32,32,256]{4,3,0,2,1:T(8,128)S(1)} %fusion, f32[2]{0:T(128)} %pad_maximum_fusion.3, f32[2,3]{0,1:T(4,128)} %bitcast.240, f32[2,3]{0,1:T(4,128)} %bitcast.238, f32[2,3]{0,1:T(4,128)} %bitcast.236, f32[2,3]{0,1:T(4,128)} %bitcast.234, f32[2,3]{0,1:T(4,128)} %bitcast.218, ...), kind=kOutput, calls=%fused_computation.9 | convolution fusion | flops 604372992 | bytes 8452848 | tf_op jit(solution)/shard_map/vrzix,vrim->zmx/dot_general | solution.py:70
  207.4 1.5 collective-permute-start
  208.9 1.3 collective-permute-start.1
  210.4 2.3 collective-permute-done.1
  213.0 36.4 %all_to_all.24 = f32[8,4,32,256]{3,2,1,0:T(8,128)} all-to-all(f32[8,4,32,256]{3,2,1,0:T(8,128)S(1)} %bitcast.178), channel_id=1, replica_groups=mesh['grp'=4,'blk'=8] {'blk'}, dimensions={0} | all-to-all | bytes 2097152 | tf_op jit(solution)/shard_map/all_to_all | solution.py:85
  249.4 51.6 %all-reduce.5.cloned.1.call-done = f32[8,4,32,256]{3,2,1,0:T(8,128)} async-done(((f32[8,4,32,256]{3,2,1,0:T(8,128)}), f32[8,4,32,256]{3,2,1,0:T(8,128)}) %all-reduce.5.cloned.1.call-update) | async-done | bytes 1048592 | tf_op jit(solution)/shard_map/psum | solution.py:86
  301.1 1.4 exponential_bitcast_fusion
  302.5 1.1 bitcast_multiply_fusion
  (361 shorter events, 79.8 us)
Async XLA Ops:
  15.5 68.4 %all-to-all-start = ((s32[8,4,2]{1,2,0:T(2,128)}), s32[8,4,2]{1,2,0:T(2,128)S(1)}, u32[]{:S(2)}, u32[]{:S(2)}) async-start(s32[8,4,2]{1,2,0:T(2,128)} %copy.106), calls=%async_computation | async-start | bytes 16384 | tf_op jit(solution)/shard_map/all_to_all | solution.py:54
  84.4 31.7 %all-to-all-start.1 = ((bf16[32,2,32,256]{3,2,1,0:T(8,128)(2,1)}), bf16[32,2,32,256]{3,2,1,0:T(8,128)(2,1)S(1)}, u32[]{:S(2)}, u32[]{:S(2)}) async-start(bf16[32,2,32,256]{3,2,1,0:T(8,128)(2,1)} %copy.110), calls=%async_computation.1 | async-start | bytes 2097152 | tf_op jit(solution)/shard_map/all_to_all | solution.py:53
  117.1 52.6 %all-to-all-start.2 = ((f32[8,4,64,256]{3,2,1,0:T(8,128)}), f32[8,4,64,256]{3,2,1,0:T(8,128)S(1)}, u32[]{:S(2)}, u32[]{:S(2)}) async-start(f32[8,4,64,256]{3,2,1,0:T(8,128)} %fusion.19), calls=%async_computation.2 | async-start | bytes 4194304 | tf_op jit(solution)/shard_map/all_to_all | solution.py:44
  120.7 180.4 %all-reduce.5.cloned.1.call-start = ((), (), s32[]{:S(2)}) async-start(), calls=%async_computation.4 | async-start | bytes 2097152 | tf_op jit(solution)/shard_map/psum | solution.py:86
  192.0 11.4 %copy-start.30 = (pred[32,64]{1,0:T(8,128)(4,1)S(1)}, pred[32,64]{1,0:T(8,128)(4,1)}, u32[]{:S(2)}) copy-start(pred[32,64]{1,0:T(8,128)(4,1)} %get-tuple-element.126) | copy-start | bytes 6148
  192.0 11.4 %copy-start.31 = (pred[32,64]{1,0:T(8,128)(4,1)S(1)}, pred[32,64]{1,0:T(8,128)(4,1)}, u32[]{:S(2)}) copy-start(pred[32,64]{1,0:T(8,128)(4,1)} %get-tuple-element.127) | copy-start | bytes 6148
  192.0 11.4 %copy-start.32 = (pred[32,64]{1,0:T(8,128)(4,1)S(1)}, pred[32,64]{1,0:T(8,128)(4,1)}, u32[]{:S(2)}) copy-start(pred[32,64]{1,0:T(8,128)(4,1)} %get-tuple-element.128) | copy-start | bytes 6148
  192.0 11.4 %copy-start.33 = (pred[32,64]{1,0:T(8,128)(4,1)S(1)}, pred[32,64]{1,0:T(8,128)(4,1)}, u32[]{:S(2)}) copy-start(pred[32,64]{1,0:T(8,128)(4,1)} %get-tuple-element.129) | copy-start | bytes 6148
  192.0 11.4 %copy-start.34 = (pred[32,64]{1,0:T(8,128)(4,1)S(1)}, pred[32,64]{1,0:T(8,128)(4,1)}, u32[]{:S(2)}) copy-start(pred[32,64]{1,0:T(8,128)(4,1)} %get-tuple-element.130) | copy-start | bytes 6148
  192.0 11.4 %copy-start.35 = (pred[32,64]{1,0:T(8,128)(4,1)S(1)}, pred[32,64]{1,0:T(8,128)(4,1)}, u32[]{:S(2)}) copy-start(pred[32,64]{1,0:T(8,128)(4,1)} %get-tuple-element.131) | copy-start | bytes 6148
  192.0 11.4 %copy-start.36 = (pred[32,64]{1,0:T(8,128)(4,1)S(1)}, pred[32,64]{1,0:T(8,128)(4,1)}, u32[]{:S(2)}) copy-start(pred[32,64]{1,0:T(8,128)(4,1)} %get-tuple-element.132) | copy-start | bytes 6148
  192.0 11.4 %copy-start.37 = (pred[32,64]{1,0:T(8,128)(4,1)S(1)}, pred[32,64]{1,0:T(8,128)(4,1)}, u32[]{:S(2)}) copy-start(pred[32,64]{1,0:T(8,128)(4,1)} %get-tuple-element.133) | copy-start | bytes 6148
  192.0 11.4 %copy-start.38 = (pred[32,64]{1,0:T(8,128)(4,1)S(1)}, pred[32,64]{1,0:T(8,128)(4,1)}, u32[]{:S(2)}) copy-start(pred[32,64]{1,0:T(8,128)(4,1)} %get-tuple-element.134) | copy-start | bytes 6148
  192.1 11.4 %copy-start.39 = (pred[32,64]{1,0:T(8,128)(4,1)S(1)}, pred[32,64]{1,0:T(8,128)(4,1)}, u32[]{:S(2)}) copy-start(pred[32,64]{1,0:T(8,128)(4,1)} %get-tuple-element.135) | copy-start | bytes 6148
  192.1 11.4 %copy-start.40 = (pred[32,64]{1,0:T(8,128)(4,1)S(1)}, pred[32,64]{1,0:T(8,128)(4,1)}, u32[]{:S(2)}) copy-start(pred[32,64]{1,0:T(8,128)(4,1)} %get-tuple-element.136) | copy-start | bytes 6148
  192.1 11.4 %copy-start.41 = (pred[32,64]{1,0:T(8,128)(4,1)S(1)}, pred[32,64]{1,0:T(8,128)(4,1)}, u32[]{:S(2)}) copy-start(pred[32,64]{1,0:T(8,128)(4,1)} %get-tuple-element.137) | copy-start | bytes 6148
  192.1 11.4 %copy-start.42 = (pred[32,64]{1,0:T(8,128)(4,1)S(1)}, pred[32,64]{1,0:T(8,128)(4,1)}, u32[]{:S(2)}) copy-start(pred[32,64]{1,0:T(8,128)(4,1)} %get-tuple-element.138) | copy-start | bytes 6148
  192.1 11.4 %copy-start.43 = (pred[32,64]{1,0:T(8,128)(4,1)S(1)}, pred[32,64]{1,0:T(8,128)(4,1)}, u32[]{:S(2)}) copy-start(pred[32,64]{1,0:T(8,128)(4,1)} %get-tuple-element.139) | copy-start | bytes 6148
  192.1 11.4 %copy-start.44 = (pred[32,64]{1,0:T(8,128)(4,1)S(1)}, pred[32,64]{1,0:T(8,128)(4,1)}, u32[]{:S(2)}) copy-start(pred[32,64]{1,0:T(8,128)(4,1)} %get-tuple-element.140) | copy-start | bytes 6148
  192.1 11.4 %copy-start.45 = (pred[32,64]{1,0:T(8,128)(4,1)S(1)}, pred[32,64]{1,0:T(8,128)(4,1)}, u32[]{:S(2)}) copy-start(pred[32,64]{1,0:T(8,128)(4,1)} %get-tuple-element.141) | copy-start | bytes 6148
  192.1 11.4 %copy-start.46 = (pred[32,64]{1,0:T(8,128)(4,1)S(1)}, pred[32,64]{1,0:T(8,128)(4,1)}, u32[]{:S(2)}) copy-start(pred[32,64]{1,0:T(8,128)(4,1)} %get-tuple-element.142) | copy-start | bytes 6148
  192.1 11.4 %copy-start.47 = (pred[32,64]{1,0:T(8,128)(4,1)S(1)}, pred[32,64]{1,0:T(8,128)(4,1)}, u32[]{:S(2)}) copy-start(pred[32,64]{1,0:T(8,128)(4,1)} %get-tuple-element.143) | copy-start | bytes 6148
  207.4 3.0 collective-permute-start
  208.9 3.8 %collective-permute-start.1 = (f32[32,16,256]{2,1,0:T(8,128)S(1)}, f32[32,16,256]{2,1,0:T(8,128)S(1)}, u32[]{:S(2)}, u32[]{:S(2)}) collective-permute-start(f32[32,16,256]{2,1,0:T(8,128)S(1)} %get-tuple-element.44), channel_id=1, source_target_pairs={{1,0},{2,1},{3,2},{4,3},{5,4},{6,5},{7,6},{9,8},{10,9},{11,10},{12... | collective-permute-start | bytes 1572872 | tf_op jit(solution)/shard_map/ppermute | solution.py:77
  (85 other events, 584.3 us)
Sparse Core Ops, SparseCore 0:
  249.5 51.4 all-reduce.4
where the time goes:
time: 316 us; the launch traced here: 311 us
  waiting for transfers between devices  108 us (34%)
  local copies, waits for them, and re-layouts  59.3 us (19%)
  matrix products  39.1 us (12%)
  blocking collectives  36.4 us (12%)
  other arithmetic  28.5 us (9%)
  between operations  21.6 us (7%)
  starting transfers between devices  18.3 us (6%)
    psum x1, waiting for transfers between devices, shards(): summed = lax.psum(logs, 'grp')  51.6 us
    broadcast_in_dim x62, local copies, waits for them, and re-layouts, band(): out = jnp.where(shift == t, taps[..., t, None, None], out)  42.3 us
    all_to_all x1, blocking collectives, shards(): lax.all_to_all(logs.reshape(blocks, cz, py, nx), 'blk', 0, 0, tiled=True)  36.4 us
    all_to_all x1, waiting for transfers between devices, shards(): lax.all_to_all(windows, 'blk', 0, 0, tiled=True).reshape(nz, ext, nx)  32.7 us
    all_to_all x1, waiting for transfers between devices, shards(): got = lax.all_to_all(send, 'blk', 0, 0, tiled=True)  20.7 us
    eq x48, other arithmetic, band(): out = jnp.where(shift == t, taps[..., t, None, None], out)  18.7 us
    dot_general x1, matrix products, shards(): a = jnp.einsum('vrzin,vrnx->vrzix', a, bx, precision=HIGH)  11 us
    dot_general x1, matrix products, shards(): t = jnp.einsum('vrzix,vrnx->vrzin', t, bx, precision=HIGH)  10.7 us
  transfers between devices with their start and end apart: 6, of which 5 were waited for; matrix products, arithmetic and copies ran while one was open for 26% of the time, Pallas kernels for 0%

commit v1 on v0

--- a/solution.py
+++ b/solution.py
@@ -5,6 +5,29 @@
 
 VSLOT = 2
 HIGH = lax.Precision.HIGH
+
+
+def split_up(x, dim, devices):
+    shape = x.shape
+    pieces = x.reshape(*shape[:dim], devices, shape[dim] // devices, *shape[dim + 1 :])
+    return jnp.moveaxis(pieces, dim, 0)
+
+
+def joined_along(pieces, dim):
+    pieces = jnp.moveaxis(pieces, 0, dim)
+    shape = pieces.shape
+    return pieces.reshape(*shape[:dim], shape[dim] * shape[dim + 1], *shape[dim + 2 :])
+
+
+def exchange_directly(x, axis, split_dim, concat_dim):
+    size, index = (lax.axis_size(axis), lax.axis_index(axis))
+    blocks = split_up(x, split_dim, size)
+    finished = [blocks[index]]
+    for step in range(1, size):
+        sent = blocks[(index + step) % size]
+        finished.append(lax.ppermute(sent, axis, [(i, (i + step) % size) for i in range(size)]))
+    blocks = jnp.stack(finished)[(index - jnp.arange(size)) % size]
+    return joined_along(blocks, concat_dim)
 
 
 def band(taps, rows, cols, lead):
@@ -82,7 +105,7 @@
             + jnp.pad(down, ((0, 0), (rest, 0), (0, 0)))
         )
     logs = jnp.log(average)
-    logs = lax.all_to_all(logs.reshape(blocks, cz, py, nx), "blk", 0, 0, tiled=True)
+    logs = exchange_directly(logs.reshape(blocks, cz, py, nx), "blk", 0, 0)
     summed = lax.psum(logs, "grp")
     summed = jnp.transpose(summed, (1, 0, 2, 3)).reshape(cz, ny, nx)
     return estimate * jnp.exp(summed / groups)

time: 316 us -> 316 us (level)
  blocking collectives: 36.4 us -> 0 us
  starting transfers between devices: 18.3 us -> 36 us
  waiting for transfers between devices: 108 us -> 123 us
    all_to_all x1 -> x0, blocking collectives: 36.4 us -> none  [shards(): lax.all_to_all(logs.reshape(blocks, cz, py, nx), 'blk', 0, 0, tiled=True)]
    ppermute x0 -> x7, starting transfers between devices: none -> 16.9 us  [exchange_directly(): lax.ppermute(sent, axis, [(i, (i + step) % size) for i in range(size)])]
    psum x1, waiting for transfers between devices: 51.6 us -> 61 us  [shards(): summed = lax.psum(logs, 'grp')]
    ppermute x0 -> x7, waiting for transfers between devices: none -> 6.16 us  [exchange_directly(): lax.ppermute(sent, axis, [(i, (i + step) % size) for i in range(size)])]
    unnamed x215 -> x221, local copies, waits for them, and re-layouts: 7.62 us -> 7.77 us
  transfers between devices with their start and end apart: 6 -> 13, of which waited for: 5 -> 6; matrix products, arithmetic and copies ran while one was open for 26% -> 26% of each run, Pallas kernels for 0% -> 0%
where the time goes in v1:
time: 316 us; the launch traced here: 311 us
  waiting for transfers between devices  123 us (39%)
  local copies, waits for them, and re-layouts  62.1 us (20%)
  matrix products  39 us (12%)
  starting transfers between devices  36 us (11%)
  other arithmetic  29.6 us (9%)
  between operations  21.3 us (7%)
    psum x1, waiting for transfers between devices, shards(): summed = lax.psum(logs, 'grp')  61 us
    broadcast_in_dim x62, local copies, waits for them, and re-layouts, band(): out = jnp.where(shift == t, taps[..., t, None, None], out)  42.3 us
    all_to_all x1, waiting for transfers between devices, shards(): lax.all_to_all(windows, 'blk', 0, 0, tiled=True).reshape(nz, ext, nx)  32.6 us
    all_to_all x1, waiting for transfers between devices, shards(): got = lax.all_to_all(send, 'blk', 0, 0, tiled=True)  20.6 us
    eq x48, other arithmetic, band(): out = jnp.where(shift == t, taps[..., t, None, None], out)  18.7 us
    ppermute x7, starting transfers between devices, exchange_directly(): lax.ppermute(sent, axis, [(i, (i + step) % size) for i in range(size)])  16.9 us
    dot_general x1, matrix products, shards(): a = jnp.einsum('vrzin,vrnx->vrzix', a, bx, precision=HIGH)  10.8 us
    dot_general x1, matrix products, shards(): t = jnp.einsum('vrzix,vrnx->vrzin', t, bx, precision=HIGH)  10.7 us
  transfers between devices with their start and end apart: 13, of which 6 were waited for; matrix products, arithmetic and copies ran while one was open for 26% of the time, Pallas kernels for 0%

profile of v1, /device:TPU:0, one launch (start us, length us, event | category | flops | bytes accessed | tf_op | source)
XLA Modules:
  0.0 311.2 jit_solution(16551723360989452251)
XLA Ops:
  15.1 6.4 %all-to-all-start = ((s32[8,4,2]{1,2,0:T(2,128)}), s32[8,4,2]{1,2,0:T(2,128)S(1)}, u32[]{:S(2)}, u32[]{:S(2)}) async-start(s32[8,4,2]{1,2,0:T(2,128)} %copy.106), calls=%async_computation | async-start | bytes 16384 | tf_op jit(solution)/shard_map/all_to_all | solution.py:77
  79.7 1.6 copy.110
  83.9 5.1 %all-to-all-start.1 = ((bf16[32,2,32,256]{3,2,1,0:T(8,128)(2,1)}), bf16[32,2,32,256]{3,2,1,0:T(8,128)(2,1)S(1)}, u32[]{:S(2)}, u32[]{:S(2)}) async-start(bf16[32,2,32,256]{3,2,1,0:T(8,128)(2,1)} %copy.110), calls=%async_computation.1 | async-start | bytes 2097152 | tf_op jit(solution)/shard_map/all_to_all | solution.py:76
  94.9 20.6 %all-to-all-done.1 = bf16[32,2,32,256]{3,2,1,0:T(8,128)(2,1)S(1)} async-done(((bf16[32,2,32,256]{3,2,1,0:T(8,128)(2,1)}), bf16[32,2,32,256]{3,2,1,0:T(8,128)(2,1)S(1)}, u32[]{:S(2)}, u32[]{:S(2)}) %all-to-all-start.1) | async-done | bytes 1048608 | tf_op jit(solution)/shard_map/all_to_all | solution.py:76
  116.5 3.6 %all-to-all-start.2 = ((f32[8,4,64,256]{3,2,1,0:T(8,128)}), f32[8,4,64,256]{3,2,1,0:T(8,128)S(1)}, u32[]{:S(2)}, u32[]{:S(2)}) async-start(f32[8,4,64,256]{3,2,1,0:T(8,128)} %fusion.19), calls=%async_computation.2 | async-start | bytes 4194304 | tf_op jit(solution)/shard_map/all_to_all | solution.py:67
  133.5 2.9 fusion.14
  136.5 32.6 %all-to-all-done.2 = f32[8,4,64,256]{3,2,1,0:T(8,128)S(1)} async-done(((f32[8,4,64,256]{3,2,1,0:T(8,128)}), f32[8,4,64,256]{3,2,1,0:T(8,128)S(1)}, u32[]{:S(2)}, u32[]{:S(2)}) %all-to-all-start.2) | async-done | bytes 2097184 | tf_op jit(solution)/shard_map/all_to_all | solution.py:67
  169.3 4.2 %convolution_bitcast_fusion = f32[2,3,32,32,256]{4,3,2,1,0:T(8,128)S(1)} fusion(f32[32,64,256,1,1]{2,1,0,4,3:T(8,128)S(1)} %bitcast.208, f32[2,3]{0,1:T(4,128)} %bitcast.271, pred[32,64]{1,0:T(8,128)(4,1)S(1)} %get-tuple-element.129, f32[2,3]{0,1:T(4,128)} %bitcast.269, pred[32,64]{1,0:T(8,128)(4,1)S(1)} %get-tuple-element.130, f32[2,3]{0,1:T(4,128)} %bitcast.267, ...), kind=kOutput, calls=%fused_computation.5 | convolution fusion | flops 604360704 | bytes 8452840 | tf_op jit(solution)/shard_map/zmx,vrim->vrzix/dot_general | solution.py:87
  174.0 10.7 %fusion.2 = f32[2,3,32,32,256]{4,2,1,3,0:T(8,128)S(1)} fusion(f32[2,3,32,32,256]{4,3,2,1,0:T(8,128)S(1)} %convolution_bitcast_fusion, f32[2,3]{0,1:T(4,128)} %bitcast.334, pred[256,256]{1,0:T(8,128)(4,1)S(1)} %get-tuple-element.159, f32[2,3]{0,1:T(4,128)} %bitcast.332, pred[256,256]{1,0:T(8,128)(4,1)S(1)} %get-tuple-element.160, f32[2,3]{0,1:T(4,128)} %bitcast.330, ...), kind=kOutput, calls=%fused_computation.3 | convolution fusion | flops 2428108800 | bytes 14615272 | tf_op jit(solution)/shard_map/vrzix,vrnx->vrzin/dot_general | solution.py:88
  185.1 3.3 %fusion.51 = f32[2,32,32,256,1]{3,1,4,2,0:T(8,128)S(1)} fusion(f32[2,3,32,32,256]{4,2,1,3,0:T(8,128)S(1)} %fusion.2, f32[2,3]{1,0:T(2,128)} %get-tuple-element.34, f32[2,3]{1,0:T(2,128)} %get-tuple-element.35, f32[2,3]{1,0:T(2,128)} %get-tuple-element.33, f32[2,3]{1,0:T(2,128)} %get-tuple-element.32, f32[2,3]{1,0:T(2,128)} %get-tuple-element.31, ...), kind=kOutput, calls=%fused_computation.84 | convolution fusion | flops 302180352 | bytes 8421096 | tf_op jit(solution)/shard_map/vrzin,vrpz->vpin/dot_general | solution.py:89
  188.6 2.9 fusion.4
  191.9 10.8 %fusion = f32[2,3,32,32,256]{4,3,0,2,1:T(8,128)S(1)} fusion(f32[2,3,32,32,256]{4,2,3,1,0:T(8,128)S(1)} %fusion.4, f32[2,3]{0,1:T(4,128)} %bitcast.335, f32[2,3]{0,1:T(4,128)} %bitcast.333, f32[2,3]{0,1:T(4,128)} %bitcast.331, f32[2,3]{0,1:T(4,128)} %bitcast.329, f32[2,3]{0,1:T(4,128)} %bitcast.327, f32[2,3]{0,1:T(4,128)} %bitcast.325, f32[2,3]{0,1:T(4,128)} %bitcast.323, ...), kind=kOutput, calls=%fused_computation.1 | convolution fusion | flops 2428108800 | bytes 14615272 | tf_op jit(solution)/shard_map/vrzin,vrnx->vrzix/dot_general | solution.py:92
  203.1 3.6 %convolution_bitcast_fusion.1 = f32[32,64,256]{2,1,0:T(8,128)S(1)} fusion(f32[2,3,32,32,256]{4,3,0,2,1:T(8,128)S(1)} %fusion, f32[2]{0:T(128)} %pad_maximum_fusion.3, f32[2,3]{0,1:T(4,128)} %bitcast.272, f32[2,3]{0,1:T(4,128)} %bitcast.270, f32[2,3]{0,1:T(4,128)} %bitcast.268, f32[2,3]{0,1:T(4,128)} %bitcast.266, f32[2,3]{0,1:T(4,128)} %bitcast.250, ...), kind=kOutput, calls=%fused_computation.10 | convolution fusion | flops 604372992 | bytes 8452848 | tf_op jit(solution)/shard_map/vrzix,vrim->zmx/dot_general | solution.py:93
  207.8 2.2 collective-permute-start
  211.5 2.7 collective-permute-done.1
  214.2 1.4 fusion.10
  215.7 6.0 %collective-permute-start.2 = (f32[1,4,32,256]{3,2,1,0:T(8,128)S(1)}, f32[1,4,32,256]{3,2,1,0:T(8,128)S(1)}, u32[]{:S(2)}, u32[]{:S(2)}) collective-permute-start(f32[1,4,32,256]{3,2,1,0:T(8,128)S(1)} %get-tuple-element.51), channel_id=1, source_target_pairs={{0,1},{1,2},{2,3},{3,4},{4,5},{5,6},{6,7},{7,0},{8,9},{9,10},{10,1... | collective-permute-start | bytes 393224 | tf_op jit(solution)/shard_map/ppermute | solution.py:28
  222.5 2.9 collective-permute-start.4
  225.7 2.3 collective-permute-start.6
  228.0 2.9 collective-permute-start.7
  230.8 1.9 collective-permute-start.8
  232.7 6.0 %collective-permute-done.4 = f32[1,4,32,256]{3,2,1,0:T(8,128)S(1)} collective-permute-done((f32[1,4,32,256]{3,2,1,0:T(8,128)S(1)}, f32[1,4,32,256]{3,2,1,0:T(8,128)S(1)}, u32[]{:S(2)}, u32[]{:S(2)}) %collective-permute-start.4) | collective-permute-done | bytes 131104 | tf_op jit(solution)/shard_map/ppermute | solution.py:28
  239.0 1.6 gather_fusion
  240.6 61.0 %all-reduce.5.cloned.1.call-done = f32[8,4,32,256]{3,2,1,0:T(8,128)} async-done(((f32[8,4,32,256]{3,2,1,0:T(8,128)}), f32[8,4,32,256]{3,2,1,0:T(8,128)}) %all-reduce.5.cloned.1.call-update) | async-done | bytes 1048592 | tf_op jit(solution)/shard_map/psum | solution.py:109
  (385 shorter events, 90.6 us)
Async XLA Ops:
  15.1 68.2 %all-to-all-start = ((s32[8,4,2]{1,2,0:T(2,128)}), s32[8,4,2]{1,2,0:T(2,128)S(1)}, u32[]{:S(2)}, u32[]{:S(2)}) async-start(s32[8,4,2]{1,2,0:T(2,128)} %copy.106), calls=%async_computation | async-start | bytes 16384 | tf_op jit(solution)/shard_map/all_to_all | solution.py:77
  83.9 31.7 %all-to-all-start.1 = ((bf16[32,2,32,256]{3,2,1,0:T(8,128)(2,1)}), bf16[32,2,32,256]{3,2,1,0:T(8,128)(2,1)S(1)}, u32[]{:S(2)}, u32[]{:S(2)}) async-start(bf16[32,2,32,256]{3,2,1,0:T(8,128)(2,1)} %copy.110), calls=%async_computation.1 | async-start | bytes 2097152 | tf_op jit(solution)/shard_map/all_to_all | solution.py:76
  116.5 52.6 %all-to-all-start.2 = ((f32[8,4,64,256]{3,2,1,0:T(8,128)}), f32[8,4,64,256]{3,2,1,0:T(8,128)S(1)}, u32[]{:S(2)}, u32[]{:S(2)}) async-start(f32[8,4,64,256]{3,2,1,0:T(8,128)} %fusion.19), calls=%async_computation.2 | async-start | bytes 4194304 | tf_op jit(solution)/shard_map/all_to_all | solution.py:67
  120.1 181.5 %all-reduce.5.cloned.1.call-start = ((), (), s32[]{:S(2)}) async-start(), calls=%async_computation.3 | async-start | bytes 2097152 | tf_op jit(solution)/shard_map/psum | solution.py:109
  191.5 11.2 %copy-start.30 = (pred[32,64]{1,0:T(8,128)(4,1)S(1)}, pred[32,64]{1,0:T(8,128)(4,1)}, u32[]{:S(2)}) copy-start(pred[32,64]{1,0:T(8,128)(4,1)} %get-tuple-element.134) | copy-start | bytes 6148
  191.5 11.2 %copy-start.31 = (pred[32,64]{1,0:T(8,128)(4,1)S(1)}, pred[32,64]{1,0:T(8,128)(4,1)}, u32[]{:S(2)}) copy-start(pred[32,64]{1,0:T(8,128)(4,1)} %get-tuple-element.135) | copy-start | bytes 6148
  191.5 11.2 %copy-start.32 = (pred[32,64]{1,0:T(8,128)(4,1)S(1)}, pred[32,64]{1,0:T(8,128)(4,1)}, u32[]{:S(2)}) copy-start(pred[32,64]{1,0:T(8,128)(4,1)} %get-tuple-element.136) | copy-start | bytes 6148
  191.6 11.2 %copy-start.33 = (pred[32,64]{1,0:T(8,128)(4,1)S(1)}, pred[32,64]{1,0:T(8,128)(4,1)}, u32[]{:S(2)}) copy-start(pred[32,64]{1,0:T(8,128)(4,1)} %get-tuple-element.137) | copy-start | bytes 6148
  191.6 11.2 %copy-start.34 = (pred[32,64]{1,0:T(8,128)(4,1)S(1)}, pred[32,64]{1,0:T(8,128)(4,1)}, u32[]{:S(2)}) copy-start(pred[32,64]{1,0:T(8,128)(4,1)} %get-tuple-element.138) | copy-start | bytes 6148
  191.6 11.2 %copy-start.35 = (pred[32,64]{1,0:T(8,128)(4,1)S(1)}, pred[32,64]{1,0:T(8,128)(4,1)}, u32[]{:S(2)}) copy-start(pred[32,64]{1,0:T(8,128)(4,1)} %get-tuple-element.139) | copy-start | bytes 6148
  191.6 11.2 %copy-start.36 = (pred[32,64]{1,0:T(8,128)(4,1)S(1)}, pred[32,64]{1,0:T(8,128)(4,1)}, u32[]{:S(2)}) copy-start(pred[32,64]{1,0:T(8,128)(4,1)} %get-tuple-element.140) | copy-start | bytes 6148
  191.6 11.2 %copy-start.37 = (pred[32,64]{1,0:T(8,128)(4,1)S(1)}, pred[32,64]{1,0:T(8,128)(4,1)}, u32[]{:S(2)}) copy-start(pred[32,64]{1,0:T(8,128)(4,1)} %get-tuple-element.141) | copy-start | bytes 6148
  191.6 11.2 %copy-start.38 = (pred[32,64]{1,0:T(8,128)(4,1)S(1)}, pred[32,64]{1,0:T(8,128)(4,1)}, u32[]{:S(2)}) copy-start(pred[32,64]{1,0:T(8,128)(4,1)} %get-tuple-element.142) | copy-start | bytes 6148
  191.6 11.2 %copy-start.39 = (pred[32,64]{1,0:T(8,128)(4,1)S(1)}, pred[32,64]{1,0:T(8,128)(4,1)}, u32[]{:S(2)}) copy-start(pred[32,64]{1,0:T(8,128)(4,1)} %get-tuple-element.143) | copy-start | bytes 6148
  191.6 11.2 %copy-start.40 = (pred[32,64]{1,0:T(8,128)(4,1)S(1)}, pred[32,64]{1,0:T(8,128)(4,1)}, u32[]{:S(2)}) copy-start(pred[32,64]{1,0:T(8,128)(4,1)} %get-tuple-element.144) | copy-start | bytes 6148
  207.8 3.6 %collective-permute-start = (f32[32,16,256]{2,1,0:T(8,128)}, f32[32,16,256]{2,1,0:T(8,128)}, u32[]{:S(2)}, u32[]{:S(2)}) collective-permute-start(f32[32,16,256]{2,1,0:T(8,128)} %get-tuple-element.43), channel_id=1, source_target_pairs={{0,1},{1,2},{2,3},{3,4},{4,5},{5,6},{6,7},{8,9},{9,10},{10,11},{11... | collective-permute-start | bytes 1572872 | tf_op jit(solution)/shard_map/ppermute | solution.py:99
  210.1 4.1 %collective-permute-start.1 = (f32[32,16,256]{2,1,0:T(8,128)}, f32[32,16,256]{2,1,0:T(8,128)}, u32[]{:S(2)}, u32[]{:S(2)}) collective-permute-start(f32[32,16,256]{2,1,0:T(8,128)} %get-tuple-element.44), channel_id=1, source_target_pairs={{1,0},{2,1},{3,2},{4,3},{5,4},{6,5},{7,6},{9,8},{10,9},{11,10},{12... | collective-permute-start | bytes 1572872 | tf_op jit(solution)/shard_map/ppermute | solution.py:100
  215.7 12.3 %collective-permute-start.2 = (f32[1,4,32,256]{3,2,1,0:T(8,128)S(1)}, f32[1,4,32,256]{3,2,1,0:T(8,128)S(1)}, u32[]{:S(2)}, u32[]{:S(2)}) collective-permute-start(f32[1,4,32,256]{3,2,1,0:T(8,128)S(1)} %get-tuple-element.51), channel_id=1, source_target_pairs={{0,1},{1,2},{2,3},{3,4},{4,5},{5,6},{6,7},{7,0},{8,9},{9,10},{10,1... | collective-permute-start | bytes 393224 | tf_op jit(solution)/shard_map/ppermute | solution.py:28
  221.7 9.2 %collective-permute-start.3 = (f32[1,4,32,256]{3,2,1,0:T(8,128)S(1)}, f32[1,4,32,256]{3,2,1,0:T(8,128)S(1)}, u32[]{:S(2)}, u32[]{:S(2)}) collective-permute-start(f32[1,4,32,256]{3,2,1,0:T(8,128)S(1)} %get-tuple-element.50), channel_id=1, source_target_pairs={{0,2},{1,3},{2,4},{3,5},{4,6},{5,7},{6,0},{7,1},{8,10},{9,11},{10,... | collective-permute-start | bytes 393224 | tf_op jit(solution)/shard_map/ppermute | solution.py:28
  222.5 16.2 %collective-permute-start.4 = (f32[1,4,32,256]{3,2,1,0:T(8,128)S(1)}, f32[1,4,32,256]{3,2,1,0:T(8,128)S(1)}, u32[]{:S(2)}, u32[]{:S(2)}) collective-permute-start(f32[1,4,32,256]{3,2,1,0:T(8,128)S(1)} %get-tuple-element.49), channel_id=1, source_target_pairs={{0,3},{1,4},{2,5},{3,6},{4,7},{5,0},{6,1},{7,2},{8,11},{9,12},{10,... | collective-permute-start | bytes 393224 | tf_op jit(solution)/shard_map/ppermute | solution.py:28
  225.4 13.4 %collective-permute-start.5 = (f32[1,4,32,256]{3,2,1,0:T(8,128)S(1)}, f32[1,4,32,256]{3,2,1,0:T(8,128)S(1)}, u32[]{:S(2)}, u32[]{:S(2)}) collective-permute-start(f32[1,4,32,256]{3,2,1,0:T(8,128)S(1)} %get-tuple-element.48), channel_id=1, source_target_pairs={{0,4},{1,5},{2,6},{3,7},{4,0},{5,1},{6,2},{7,3},{8,12},{9,13},{10,... | collective-permute-start | bytes 393224 | tf_op jit(solution)/shard_map/ppermute | solution.py:28
  225.7 13.2 %collective-permute-start.6 = (f32[1,4,32,256]{3,2,1,0:T(8,128)S(1)}, f32[1,4,32,256]{3,2,1,0:T(8,128)S(1)}, u32[]{:S(2)}, u32[]{:S(2)}) collective-permute-start(f32[1,4,32,256]{3,2,1,0:T(8,128)S(1)} %get-tuple-element.47), channel_id=1, source_target_pairs={{0,5},{1,6},{2,7},{3,0},{4,1},{5,2},{6,3},{7,4},{8,13},{9,14},{10,... | collective-permute-start | bytes 393224 | tf_op jit(solution)/shard_map/ppermute | solution.py:28
  228.0 11.0 %collective-permute-start.7 = (f32[1,4,32,256]{3,2,1,0:T(8,128)S(1)}, f32[1,4,32,256]{3,2,1,0:T(8,128)S(1)}, u32[]{:S(2)}, u32[]{:S(2)}) collective-permute-start(f32[1,4,32,256]{3,2,1,0:T(8,128)S(1)} %get-tuple-element.46), channel_id=1, source_target_pairs={{0,6},{1,7},{2,0},{3,1},{4,2},{5,3},{6,4},{7,5},{8,14},{9,15},{10,... | collective-permute-start | bytes 393224 | tf_op jit(solution)/shard_map/ppermute | solution.py:28
  230.8 8.1 %collective-permute-start.8 = (f32[1,4,32,256]{3,2,1,0:T(8,128)S(1)}, f32[1,4,32,256]{3,2,1,0:T(8,128)S(1)}, u32[]{:S(2)}, u32[]{:S(2)}) collective-permute-start(f32[1,4,32,256]{3,2,1,0:T(8,128)S(1)} %get-tuple-element.45), channel_id=1, source_target_pairs={{0,7},{1,0},{2,1},{3,2},{4,3},{5,4},{6,5},{7,6},{8,15},{9,8},{10,9... | collective-permute-start | bytes 393224 | tf_op jit(solution)/shard_map/ppermute | solution.py:28
  (92 other events, 662.0 us)
Sparse Core Ops, SparseCore 0:
  240.7 60.8 all-reduce.4
